TPU v7x, 32 devices: a whole 2x2x4 slice. The times are simulated.
32 devices in a mesh: groups: 2 (over y), patch: 4 (over z), sub: 2 (over x), half: 2 (over core).
Axes of the slice: x: 2, y: 2, z: 4, core: 2. Of those that a mesh axis runs over, the one named last changes fastest.
Arguments:
- vectors: float32 [2, 8192, 256], P(None, ('groups', 'patch', 'sub', 'half')), parts along dimension 1, may hold values from -600 to 600
- prestress: bfloat16 [8192, 3, 256], P(('groups', 'patch', 'sub', 'half')), parts along dimension 0, may hold values from -4 to 4
- thickness: float32 [8192, 256], P(('groups', 'patch', 'sub', 'half')), parts along dimension 0, may hold values from 0.5 to 2
- foundation: float32 [8192, 256], P(('groups', 'patch', 'sub', 'half')), parts along dimension 0, may hold values from 2 to 6
- patch_rows: int32 [64], P(('groups', 'patch', 'sub', 'half')), parts along dimension 0, may hold values from 64 to 128, as said below
- matched: int32 [64], P(('groups', 'patch', 'sub', 'half')), parts along dimension 0, may hold values from 0 to 31, as said below
- elem_row: int32 [8192], P(('groups', 'patch', 'sub', 'half')), parts along dimension 0, may hold values from 0 to 4095, as said below
Outputs:
- modes: float32 [2, 8192, 256], P(None, ('groups', 'patch', 'sub', 'half')), parts along dimension 1
There are 2 independent parts, one for each index of `groups`. A program takes and returns all parts, laid end to end along the dimension named above; each array names one. Nothing has to cross between parts.
Inputs may be any that keep to these rules, and one draw needn't show every extreme that they name: `patch_rows`: the largest value is reached by some patch in every draw. A permutation of the patches; the patch matched to a patch lies on the device with the same sub and half indices and a patch index one above or one below, cyclically. `elem_row`: a permutation of the rows; of each device's rows, those in positions k * 16 to (k + 1) * 16 - 1 belong to patches of the device with index k along patch+sub+half.
All inputs are finite; a program needn't handle non-finite values.
Results may differ from a plain program's by a relative error of at most 0.0003.
Values may be sent and summed in bfloat16 or wider, within the bound.
A program may use at most 64 MiB of HBM per device.

v0:
```python
import jax
import jax.numpy as jnp
from jax import lax
from jax.sharding import PartitionSpec as P

ITERS = 2
step_size = 1.0
norm_scale = 16.0
penalty_value = 8.0
penalty_slope = 4.0


def passed_along(array, axis, by):
    peers = lax.axis_size(axis)
    return lax.ppermute(array, axis, [(i, (i + by) % peers) for i in range(peers)])


def second_rows(field):
    padded = jnp.pad(field, [(0, 0)] * (field.ndim - 2) + [(1, 1), (0, 0)])
    return padded[..., :-2, :] - 2.0 * field + padded[..., 2:, :]


def second_cols(field):
    padded = jnp.pad(field, [(0, 0)] * (field.ndim - 1) + [(1, 1)])
    return padded[..., :-2] - 2.0 * field + padded[..., 2:]


def forward_rows(field):
    zeros = jnp.zeros_like(field[..., :1, :])
    return jnp.concatenate([field[..., 1:, :], zeros], axis=-2) - field


def backward_rows(field):
    zeros = jnp.zeros_like(field[..., :1, :])
    return jnp.concatenate([zeros, field[..., :-1, :]], axis=-2) - field


def forward_cols(field):
    zeros = jnp.zeros_like(field[..., :1])
    return jnp.concatenate([field[..., 1:], zeros], axis=-1) - field


def backward_cols(field):
    zeros = jnp.zeros_like(field[..., :1])
    return jnp.concatenate([zeros, field[..., :-1]], axis=-1) - field


def stiffness(field, live, thickness, foundation):
    bend_rows = thickness * live * second_rows(field)
    bend_cols = thickness * second_cols(field)
    return live * (foundation * field + second_rows(bend_rows) + second_cols(bend_cols))


def geometric(field, live, stress):
    along_rows = forward_rows(field)
    along_cols = forward_cols(field)
    nuu = stress[:, :, 0, :]
    nvv = stress[:, :, 1, :]
    nuv = stress[:, :, 2, :]
    total = backward_rows(nuu * along_rows + nuv * along_cols) + backward_cols(
        nvv * along_cols + nuv * along_rows
    )
    return live * total


def edges(field, lengths):

    def row_pick(index):
        where_rows = jnp.broadcast_to(
            index[None, :, None, None], (field.shape[0], field.shape[1], 1, field.shape[3])
        )
        return jnp.take_along_axis(field, where_rows, axis=2)[:, :, 0, :]

    top = jnp.stack([row_pick(lengths - 2), row_pick(lengths - 1)], axis=2)
    bottom = field[:, :, 0:2, :]
    return (top, bottom)


def interface(field, lengths, top, bottom, partner_top, partner_bottom):
    jump_top = top[:, :, 1, :] - partner_bottom[:, :, 0, :]
    slope_top = (
        top[:, :, 1, :]
        - top[:, :, 0, :]
        - (partner_bottom[:, :, 1, :] - partner_bottom[:, :, 0, :])
    )
    jump_bottom = partner_top[:, :, 1, :] - bottom[:, :, 0, :]
    slope_bottom = (
        partner_top[:, :, 1, :]
        - partner_top[:, :, 0, :]
        - (bottom[:, :, 1, :] - bottom[:, :, 0, :])
    )
    rows = jnp.arange(field.shape[2], dtype=jnp.int32)[None, :, None]
    last = lengths[:, None, None] - 1
    added = jnp.where(
        rows == last, (penalty_value * jump_top + penalty_slope * slope_top)[:, :, None, :], 0.0
    )
    added = added + jnp.where(rows == last - 1, (-penalty_slope * slope_top)[:, :, None, :], 0.0)
    added = added + jnp.where(
        rows == 0, (-penalty_value * jump_bottom + penalty_slope * slope_bottom)[:, :, None, :], 0.0
    )
    added = added + jnp.where(rows == 1, (-penalty_slope * slope_bottom)[:, :, None, :], 0.0)
    return added


def products(field, kfield, gfield):
    return jnp.stack(
        [
            jnp.sum(field[0] * kfield[0]),
            jnp.sum(field[0] * kfield[1]),
            jnp.sum(field[1] * kfield[1]),
            jnp.sum(field[0] * gfield[0]),
            jnp.sum(field[0] * gfield[1]),
            jnp.sum(field[1] * gfield[1]),
        ]
    )


def advance(field, kfield, gfield, totals, precond, cells):
    first_a = totals[0]
    cross_k = totals[1]
    second_a = totals[2]
    first_g = totals[3]
    cross_g = totals[4]
    second_g = totals[5]
    ratio = cross_k / first_a
    other = field[1] - ratio * field[0]
    other_k = kfield[1] - ratio * kfield[0]
    other_g = gfield[1] - ratio * gfield[0]
    other_a = second_a - ratio * cross_k
    other_q = second_g - 2.0 * ratio * cross_g + ratio * ratio * first_g
    first_mu = first_g / first_a
    other_mu = other_q / other_a
    new_first = (field[0] + step_size * precond * (gfield[0] - first_mu * kfield[0])) * jnp.sqrt(
        norm_scale * cells / first_a
    )
    new_other = (other + step_size * precond * (other_g - other_mu * other_k)) * jnp.sqrt(
        norm_scale * cells / other_a
    )
    return jnp.stack([new_first, new_other])


def choose(candidates, wanted, labels):
    match = labels[None, :] == wanted[:, None]
    return jnp.sum(jnp.where(match[None, :, :, None, None], candidates[:, None], 0.0), axis=2)


def per_device(vectors, prestress, thickness, foundation, patch_rows, matched, elem_row):
    owners = lax.axis_size("patch")
    inner = lax.axis_size(("sub", "half"))
    slots = patch_rows.shape[0]
    rows_dev = thickness.shape[0]
    prows = rows_dev // slots
    ncol = thickness.shape[1]
    per_peer = rows_dev // (owners * inner)
    blocks = prestress.reshape(owners, inner, per_peer, 3, ncol)
    targets = (elem_row % rows_dev).reshape(owners, inner, per_peer)
    arrived, arrived_rows = (
        lax.all_to_all(
            lax.all_to_all(blocks, "patch", split_axis=0, concat_axis=0, tiled=True),
            ("sub", "half"),
            split_axis=1,
            concat_axis=1,
            tiled=True,
        ),
        lax.all_to_all(
            lax.all_to_all(targets, "patch", split_axis=0, concat_axis=0, tiled=True),
            ("sub", "half"),
            split_axis=1,
            concat_axis=1,
            tiled=True,
        ),
    )
    placed = (
        jnp.zeros((rows_dev, 3, ncol), jnp.bfloat16)
        .at[arrived_rows.reshape(-1)]
        .set(arrived.reshape(-1, 3, ncol))
    )
    stress = placed.astype(jnp.float32).reshape(slots, prows, 3, ncol)
    rows = jnp.arange(prows, dtype=jnp.int32)[None, :]
    live = (rows < patch_rows[:, None]).astype(jnp.float32)[:, :, None]
    thick = thickness.reshape(slots, prows, ncol)
    support = foundation.reshape(slots, prows, ncol)
    precond = live / (support + 12.0 * thick)
    own_ids = lax.axis_index(("patch", "sub", "half")) * slots + jnp.arange(slots, dtype=jnp.int32)
    labels = jnp.stack([own_ids, matched])
    field = vectors.reshape(2, slots, prows, ncol) * live
    cells = jnp.float32(owners * inner * rows_dev * ncol)
    for step in range(ITERS):
        top, bottom = edges(field, patch_rows)
        strips = jnp.stack([top, bottom])
        below = passed_along((strips, labels), "patch", 1)
        above = passed_along((strips, labels), "patch", -1)
        got_strips = jnp.stack([below[0], above[0]])
        got_labels = jnp.stack([below[1], above[1]])
        count = got_strips.shape[0] * slots
        cand_top = jnp.moveaxis(got_strips[:, 0], 0, 1).reshape(2, count, 2, ncol)
        cand_bottom = jnp.moveaxis(got_strips[:, 1], 0, 1).reshape(2, count, 2, ncol)
        cand_ids = got_labels[:, 0].reshape(-1)
        cand_next = got_labels[:, 1].reshape(-1)
        partner_bottom = choose(cand_bottom, matched, cand_ids)
        partner_top = choose(cand_top, own_ids, cand_next)
        kfield = stiffness(field, live, thick, support) + interface(
            field, patch_rows, top, bottom, partner_top, partner_bottom
        )
        gfield = geometric(field, live, stress)
        totals = lax.psum(products(field, kfield, gfield), ("patch", "sub", "half"))
        field = advance(field, kfield, gfield, totals, precond, cells)
    return field.reshape(2, rows_dev, ncol)


def solution(mesh):
    in_specs = (
        P(None, ("groups", "patch", "sub", "half"), None),
        P(("groups", "patch", "sub", "half"), None, None),
        P(("groups", "patch", "sub", "half"), None),
        P(("groups", "patch", "sub", "half"), None),
        P(("groups", "patch", "sub", "half")),
        P(("groups", "patch", "sub", "half")),
        P(("groups", "patch", "sub", "half")),
    )
    out_specs = P(None, ("groups", "patch", "sub", "half"), None)
    return jax.shard_map(
        per_device, mesh=mesh, in_specs=in_specs, out_specs=out_specs, check_vma=False
    )
```

profile of v0, /device:TPU:0, one launch (start us, length us, event | category | flops | bytes accessed | tf_op | source)
XLA Modules:
  0.0 211.1 jit_solution(15988298672852159609)
XLA Ops:
  1.1 1.1 broadcast_multiply_fusion
  2.2 12.3 %gather_fusion = f32[1024]{0:T(1024)S(1)} fusion(f32[2,2,128,256]{3,2,1,0:T(8,128)S(1)} %broadcast_multiply_fusion, s32[1024]{0:T(1024)S(1)} %bitcast.210), kind=kCustom, calls=%fused_computation.clone | custom fusion | bytes 24576 | tf_op jit(solution)/shard_map/jit(take_along_axis)/gather | solution.py:72
  14.6 12.3 %gather_fusion.1 = f32[1024]{0:T(1024)S(1)} fusion(f32[2,2,128,256]{3,2,1,0:T(8,128)S(1)} %broadcast_multiply_fusion, s32[1024]{0:T(1024)S(1)} %bitcast.212), kind=kCustom, calls=%fused_computation.1.clone | custom fusion | bytes 24576 | tf_op jit(solution)/shard_map/jit(take_along_axis)/gather | solution.py:72
  27.1 3.1 %collective-permute-start.2 = (f32[2,2,2,2,256]{4,3,2,1,0:T(2,128)S(1)}, f32[2,2,2,2,256]{4,3,2,1,0:T(2,128)S(1)}, u32[]{:S(2)}, u32[]{:S(2)}) collective-permute-start(f32[2,2,2,2,256]{4,3,2,1,0:T(2,128)S(1)} %pad_maximum_fusion.4), channel_id=1, source_target_pairs={{0,4},{4,8},{8,12},{12,0},{1,5},{5,9},{9,13},{13,1},{2,6},{6,10},{... | collective-permute-start | bytes 49160 | tf_op jit(solution)/shard_map/ppermute | solution.py:15
  30.1 2.1 collective-permute-start.3
  33.0 3.8 %collective-permute-start.1 = (s32[2,2]{1,0:T(2,128)S(1)}, s32[2,2]{1,0:T(2,128)S(1)}, u32[]{:S(2)}, u32[]{:S(2)}) collective-permute-start(s32[2,2]{1,0:T(2,128)S(1)} %pad_add_fusion.4), channel_id=1, source_target_pairs={{0,12},{4,0},{8,4},{12,8},{1,13},{5,1},{9,5},{13,9},{2,14},{6,2},{... | collective-permute-start | bytes 56 | tf_op jit(solution)/shard_map/ppermute | solution.py:15
  37.5 3.2 %all-to-all-start = ((s32[4,4,16]{2,1,0:T(4,128)}), s32[4,4,16]{2,1,0:T(4,128)S(1)}, u32[]{:S(2)}, u32[]{:S(2)}) async-start(s32[4,4,16]{2,1,0:T(4,128)} %reshape.291), calls=%async_computation | async-start | bytes 16384 | tf_op jit(solution)/shard_map/all_to_all | solution.py:166
  43.8 2.4 %all-to-all-done = s32[4,4,16]{2,1,0:T(4,128)S(1)} async-done(((s32[4,4,16]{2,1,0:T(4,128)}), s32[4,4,16]{2,1,0:T(4,128)S(1)}, u32[]{:S(2)}, u32[]{:S(2)}) %all-to-all-start) | async-done | bytes 1056 | tf_op jit(solution)/shard_map/all_to_all | solution.py:166
  46.9 3.2 %all-to-all-start.1 = ((s32[4,4,16]{2,0,1:T(4,128)}), s32[4,4,16]{2,0,1:T(4,128)S(1)}, u32[]{:S(2)}, u32[]{:S(2)}) async-start(s32[4,4,16]{2,0,1:T(4,128)} %copy.28), calls=%async_computation.1 | async-start | bytes 16384 | tf_op jit(solution)/shard_map/all_to_all | solution.py:165
  50.2 3.7 %all-to-all-done.1 = s32[4,4,16]{2,0,1:T(4,128)S(1)} async-done(((s32[4,4,16]{2,0,1:T(4,128)}), s32[4,4,16]{2,0,1:T(4,128)S(1)}, u32[]{:S(2)}, u32[]{:S(2)}) %all-to-all-start.1) | async-done | bytes 1056 | tf_op jit(solution)/shard_map/all_to_all | solution.py:165
  53.9 3.5 %all-to-all-start.2 = ((bf16[4,4,16,3,256]{4,2,1,3,0:T(8,128)(2,1)}), bf16[4,4,16,3,256]{4,2,1,3,0:T(8,128)(2,1)S(1)}, u32[]{:S(2)}, u32[]{:S(2)}) async-start(bf16[4,4,16,3,256]{4,2,1,3,0:T(8,128)(2,1)} %copy.30), calls=%async_computation.2 | async-start | bytes 786432 | tf_op jit(solution)/shard_map/all_to_all | solution.py:159
  57.8 11.4 %all-to-all-done.2 = bf16[4,4,16,3,256]{4,2,1,3,0:T(8,128)(2,1)S(1)} async-done(((bf16[4,4,16,3,256]{4,2,1,3,0:T(8,128)(2,1)}), bf16[4,4,16,3,256]{4,2,1,3,0:T(8,128)(2,1)S(1)}, u32[]{:S(2)}, u32[]{:S(2)}) %all-to-all-start.2) | async-done | bytes 393248 | tf_op jit(solution)/shard_map/all_to_all | solution.py:159
  70.0 3.5 %all-to-all-start.3 = ((bf16[4,4,16,3,256]{4,2,0,3,1:T(8,128)(2,1)}), bf16[4,4,16,3,256]{4,2,0,3,1:T(8,128)(2,1)S(1)}, u32[]{:S(2)}, u32[]{:S(2)}) async-start(bf16[4,4,16,3,256]{4,2,0,3,1:T(8,128)(2,1)} %copy.31), calls=%async_computation.3 | async-start | bytes 786432 | tf_op jit(solution)/shard_map/all_to_all | solution.py:158
  73.6 7.3 %all-to-all-done.3 = bf16[4,4,16,3,256]{4,2,0,3,1:T(8,128)(2,1)S(1)} async-done(((bf16[4,4,16,3,256]{4,2,0,3,1:T(8,128)(2,1)}), bf16[4,4,16,3,256]{4,2,0,3,1:T(8,128)(2,1)S(1)}, u32[]{:S(2)}, u32[]{:S(2)}) %all-to-all-start.3) | async-done | bytes 393248 | tf_op jit(solution)/shard_map/all_to_all | solution.py:158
  81.4 7.0 %scatter_fusion = bf16[256,3,256]{2,1,0:T(4,128)(2,1)S(1)} fusion(bf16[256,3,256]{2,1,0:T(4,128)(2,1)S(1)} %broadcast_in_dim.225, s32[256]{0:T(256)S(1)} %bitcast.260, bf16[256,3,256]{2,1,0:T(4,128)(2,1)S(1)} %copy.33), kind=kCustom, calls=%fused_computation.4 | custom fusion | bytes 1180672 | tf_op jit(solution)/shard_map/scatter | solution.py:176
  89.1 1.2 copy-done.7
  93.0 3.8 %stack.135 = f32[6]{0:T(128)S(1)} concatenate(f32[1]{0:T(128)} %bitcast.30, f32[1]{0:T(128)} %bitcast.32, f32[1]{0:T(128)} %bitcast.34, f32[1]{0:T(128)} %bitcast.36, f32[1]{0:T(128)} %bitcast.38, f32[1]{0:T(128)} %bitcast.39), dimensions={0} | concatenate | bytes 48 | tf_op jit(solution)/shard_map/stack | solution.py:106
  96.8 30.2 %psum.14 = f32[6]{0:T(128)S(1)} all-reduce(f32[6]{0:T(128)S(1)} %stack.135), channel_id=1, replica_groups=mesh['groups'=2,'patch'=4,'sub'=2,'half'=2] {'patch','sub','half'}, use_global_device_ids=true, to_apply=%region_9.11 | all-reduce | flops 6 | bytes 48 | tf_op jit(solution)/shard_map/psum | solution.py:206
  136.7 12.3 %gather_fusion.3 = f32[1024]{0:T(1024)S(1)} fusion(f32[2,2,128,256]{3,2,1,0:T(8,128)S(1)} %get-tuple-element.46, s32[1024]{0:T(1024)S(1)} %bitcast.213), kind=kCustom, calls=%fused_computation.3.clone | custom fusion | bytes 24576 | tf_op jit(solution)/shard_map/jit(take_along_axis)/gather | solution.py:72
  149.1 12.3 %gather_fusion.2 = f32[1024]{0:T(1024)S(1)} fusion(f32[2,2,128,256]{3,2,1,0:T(8,128)S(1)} %get-tuple-element.46, s32[1024]{0:T(1024)S(1)} %bitcast.211), kind=kCustom, calls=%fused_computation.2.clone | custom fusion | bytes 24576 | tf_op jit(solution)/shard_map/jit(take_along_axis)/gather | solution.py:72
  161.6 3.8 %collective-permute-start.5 = (f32[2,2,2,2,256]{4,3,2,1,0:T(2,128)S(1)}, f32[2,2,2,2,256]{4,3,2,1,0:T(2,128)S(1)}, u32[]{:S(2)}, u32[]{:S(2)}) collective-permute-start(f32[2,2,2,2,256]{4,3,2,1,0:T(2,128)S(1)} %pad_maximum_fusion.5), channel_id=1, source_target_pairs={{0,12},{4,0},{8,4},{12,8},{1,13},{5,1},{9,5},{13,9},{2,14},{6,2},{... | collective-permute-start | bytes 49160 | tf_op jit(solution)/shard_map/ppermute | solution.py:15
  166.1 1.1 collective-permute-done.4
  169.5 3.8 %stack.150 = f32[6]{0:T(128)S(1)} concatenate(f32[1]{0:T(128)} %bitcast.59, f32[1]{0:T(128)} %bitcast.61, f32[1]{0:T(128)} %bitcast.62, f32[1]{0:T(128)} %bitcast.64, f32[1]{0:T(128)} %bitcast.66, f32[1]{0:T(128)} %bitcast.67), dimensions={0} | concatenate | bytes 48 | tf_op jit(solution)/shard_map/stack | solution.py:106
  173.4 29.5 %psum.15 = f32[6]{0:T(128)S(1)} all-reduce(f32[6]{0:T(128)S(1)} %stack.150), channel_id=1, replica_groups=mesh['groups'=2,'patch'=4,'sub'=2,'half'=2] {'patch','sub','half'}, use_global_device_ids=true, to_apply=%region_18.20 | all-reduce | flops 6 | bytes 48 | tf_op jit(solution)/shard_map/psum | solution.py:206
  (130 shorter events, 19.5 us)
Async XLA Ops:
  0.0 0.7 copy-start.12
  27.1 30.4 %collective-permute-start.2 = (f32[2,2,2,2,256]{4,3,2,1,0:T(2,128)S(1)}, f32[2,2,2,2,256]{4,3,2,1,0:T(2,128)S(1)}, u32[]{:S(2)}, u32[]{:S(2)}) collective-permute-start(f32[2,2,2,2,256]{4,3,2,1,0:T(2,128)S(1)} %pad_maximum_fusion.4), channel_id=1, source_target_pairs={{0,4},{4,8},{8,12},{12,0},{1,5},{5,9},{9,13},{13,1},{2,6},{6,10},{... | collective-permute-start | bytes 49160 | tf_op jit(solution)/shard_map/ppermute | solution.py:15
  30.1 27.3 %collective-permute-start.3 = (f32[2,2,2,2,256]{4,3,2,1,0:T(2,128)S(1)}, f32[2,2,2,2,256]{4,3,2,1,0:T(2,128)S(1)}, u32[]{:S(2)}, u32[]{:S(2)}) collective-permute-start(f32[2,2,2,2,256]{4,3,2,1,0:T(2,128)S(1)} %pad_maximum_fusion.4), channel_id=1, source_target_pairs={{0,12},{4,0},{8,4},{12,8},{1,13},{5,1},{9,5},{13,9},{2,14},{6,2},{... | collective-permute-start | bytes 49160 | tf_op jit(solution)/shard_map/ppermute | solution.py:15
  32.2 0.7 copy-start.13
  32.9 3.9 %copy-start.11 = (s32[256]{0:T(256)S(1)}, s32[256]{0:T(256)}, u32[]{:S(2)}) copy-start(s32[256]{0:T(256)} %param.15) | copy-start | bytes 3076
  32.9 10.7 %collective-permute-start = (s32[2,2]{1,0:T(2,128)S(1)}, s32[2,2]{1,0:T(2,128)S(1)}, u32[]{:S(2)}, u32[]{:S(2)}) collective-permute-start(s32[2,2]{1,0:T(2,128)S(1)} %pad_add_fusion.4), channel_id=1, source_target_pairs={{0,4},{4,8},{8,12},{12,0},{1,5},{5,9},{9,13},{13,1},{2,6},{6,10},{... | collective-permute-start | bytes 56 | tf_op jit(solution)/shard_map/ppermute | solution.py:15
  33.0 10.6 %collective-permute-start.1 = (s32[2,2]{1,0:T(2,128)S(1)}, s32[2,2]{1,0:T(2,128)S(1)}, u32[]{:S(2)}, u32[]{:S(2)}) collective-permute-start(s32[2,2]{1,0:T(2,128)S(1)} %pad_add_fusion.4), channel_id=1, source_target_pairs={{0,12},{4,0},{8,4},{12,8},{1,13},{5,1},{9,5},{13,9},{2,14},{6,2},{... | collective-permute-start | bytes 56 | tf_op jit(solution)/shard_map/ppermute | solution.py:15
  37.5 8.8 %all-to-all-start = ((s32[4,4,16]{2,1,0:T(4,128)}), s32[4,4,16]{2,1,0:T(4,128)S(1)}, u32[]{:S(2)}, u32[]{:S(2)}) async-start(s32[4,4,16]{2,1,0:T(4,128)} %reshape.291), calls=%async_computation | async-start | bytes 16384 | tf_op jit(solution)/shard_map/all_to_all | solution.py:166
  40.8 1.1 copy-start
  41.8 1.0 copy-start.10
  46.9 7.0 %all-to-all-start.1 = ((s32[4,4,16]{2,0,1:T(4,128)}), s32[4,4,16]{2,0,1:T(4,128)S(1)}, u32[]{:S(2)}, u32[]{:S(2)}) async-start(s32[4,4,16]{2,0,1:T(4,128)} %copy.28), calls=%async_computation.1 | async-start | bytes 16384 | tf_op jit(solution)/shard_map/all_to_all | solution.py:165
  53.9 15.4 %all-to-all-start.2 = ((bf16[4,4,16,3,256]{4,2,1,3,0:T(8,128)(2,1)}), bf16[4,4,16,3,256]{4,2,1,3,0:T(8,128)(2,1)S(1)}, u32[]{:S(2)}, u32[]{:S(2)}) async-start(bf16[4,4,16,3,256]{4,2,1,3,0:T(8,128)(2,1)} %copy.30), calls=%async_computation.2 | async-start | bytes 786432 | tf_op jit(solution)/shard_map/all_to_all | solution.py:159
  70.0 10.9 %all-to-all-start.3 = ((bf16[4,4,16,3,256]{4,2,0,3,1:T(8,128)(2,1)}), bf16[4,4,16,3,256]{4,2,0,3,1:T(8,128)(2,1)S(1)}, u32[]{:S(2)}, u32[]{:S(2)}) async-start(bf16[4,4,16,3,256]{4,2,0,3,1:T(8,128)(2,1)} %copy.31), calls=%async_computation.3 | async-start | bytes 786432 | tf_op jit(solution)/shard_map/all_to_all | solution.py:158
  89.0 1.2 copy-start.7
  89.0 1.6 copy-start.2
  89.0 1.6 copy-start.4
  90.2 0.9 copy-start.1
  90.2 1.1 copy-start.6
  135.5 1.0 copy-start.3
  135.5 1.0 copy-start.5
  161.6 5.6 %collective-permute-start.4 = (f32[2,2,2,2,256]{4,3,2,1,0:T(2,128)S(1)}, f32[2,2,2,2,256]{4,3,2,1,0:T(2,128)S(1)}, u32[]{:S(2)}, u32[]{:S(2)}) collective-permute-start(f32[2,2,2,2,256]{4,3,2,1,0:T(2,128)S(1)} %pad_maximum_fusion.5), channel_id=1, source_target_pairs={{0,4},{4,8},{8,12},{12,0},{1,5},{5,9},{9,13},{13,1},{2,6},{6,10},{... | collective-permute-start | bytes 49160 | tf_op jit(solution)/shard_map/ppermute | solution.py:15
  161.6 5.5 %collective-permute-start.5 = (f32[2,2,2,2,256]{4,3,2,1,0:T(2,128)S(1)}, f32[2,2,2,2,256]{4,3,2,1,0:T(2,128)S(1)}, u32[]{:S(2)}, u32[]{:S(2)}) collective-permute-start(f32[2,2,2,2,256]{4,3,2,1,0:T(2,128)S(1)} %pad_maximum_fusion.5), channel_id=1, source_target_pairs={{0,12},{4,0},{8,4},{12,8},{1,13},{5,1},{9,5},{13,9},{2,14},{6,2},{... | collective-permute-start | bytes 49160 | tf_op jit(solution)/shard_map/ppermute | solution.py:15
  167.6 1.0 copy-start.8
  167.7 1.0 copy-start.9
where the time goes:
time: 212 us; the launch traced here: 211 us
  local copies, waits for them, and re-layouts  75.2 us (35%)
  blocking collectives  59.7 us (28%)
  starting transfers between devices  26.3 us (12%)
  waiting for transfers between devices  26 us (12%)
  between operations  13.6 us (6%)
  other arithmetic  10.3 us (5%)
    psum x2, blocking collectives, per_device(): totals = lax.psum(products(field, kfield, gfield), ('patch', 'sub', 'half'))  59.7 us
    gather x4, local copies, waits for them, and re-layouts, row_pick(): return jnp.take_along_axis(field, where_rows, axis=2)[:, :, 0, :]  49.2 us
    ppermute x6, starting transfers between devices, passed_along(): lax.ppermute(array, axis, [(i, (i + by) % peers) for i in range(peers)])  12.9 us
    all_to_all x1, waiting for transfers between devices, per_device(): lax.all_to_all(blocks, 'patch', split_axis=0, concat_axis=0, tiled=True)  11.4 us
    another operation x2, local copies, waits for them, and re-layouts, products(): jnp.stack([jnp.sum(field[0] * kfield[0]), jnp.sum(field[0] * kfield[1]),...  7.63 us
    all_to_all x1, waiting for transfers between devices, per_device(): lax.all_to_all(lax.all_to_all(blocks, 'patch', split_axis=0, concat_axis=...  7.33 us
    scatter x1, local copies, waits for them, and re-layouts, per_device(): placed = jnp.zeros((rows_dev, 3, ncol), jnp.bfloat16).at[arrived_rows.res...  6.97 us
    unnamed x40, local copies, waits for them, and re-layouts  4.77 us
  transfers between devices with their start and end apart: 10, of which 5 were waited for; matrix products, arithmetic and copies ran while one was open for 2% of the time, Pallas kernels for 0%

commit v1 on v0

--- a/solution.py
+++ b/solution.py
@@ -203,7 +203,9 @@
             field, patch_rows, top, bottom, partner_top, partner_bottom
         )
         gfield = geometric(field, live, stress)
-        totals = lax.psum(products(field, kfield, gfield), ("patch", "sub", "half"))
+        totals = jnp.sum(
+            lax.all_gather(products(field, kfield, gfield), ("patch", "sub", "half")), axis=0
+        )
         field = advance(field, kfield, gfield, totals, precond, cells)
     return field.reshape(2, rows_dev, ncol)
 

time: 212 us -> 214 us (level)
  waiting for transfers between devices: 26 us -> 23.6 us
    psum x2 -> x0, blocking collectives: 59.7 us -> none  [per_device(): totals = lax.psum(products(field, kfield, gfield), ('patch', 'sub', 'half'))]
    unnamed x0 -> x2, blocking collectives: none -> 59.7 us
    all_to_all x1, waiting for transfers between devices: 2.45 us -> 0.25 us  [per_device(): lax.all_to_all(targets, 'patch', split_axis=0, concat_axis=0, tiled=True)]
    unnamed x40 -> x47, local copies, waits for them, and re-layouts: 4.77 us -> 6.62 us
  transfers between devices with their start and end apart: 10 -> 10, of which waited for: 5 -> 5; matrix products, arithmetic and copies ran while one was open for 2% -> 3% of each run, Pallas kernels for 0% -> 0%
where the time goes in v1:
time: 214 us; the launch traced here: 213 us
  local copies, waits for them, and re-layouts  77.2 us (36%)
  blocking collectives  59.7 us (28%)
  starting transfers between devices  27.6 us (13%)
  waiting for transfers between devices  23.6 us (11%)
  between operations  14.2 us (7%)
  other arithmetic  10.4 us (5%)
    unnamed x2, blocking collectives  59.7 us
    gather x4, local copies, waits for them, and re-layouts, row_pick(): return jnp.take_along_axis(field, where_rows, axis=2)[:, :, 0, :]  49.2 us
    ppermute x6, starting transfers between devices, passed_along(): lax.ppermute(array, axis, [(i, (i + by) % peers) for i in range(peers)])  12.9 us
    all_to_all x1, waiting for transfers between devices, per_device(): lax.all_to_all(blocks, 'patch', split_axis=0, concat_axis=0, tiled=True)  11.2 us
    another operation x2, local copies, waits for them, and re-layouts, products(): jnp.stack([jnp.sum(field[0] * kfield[0]), jnp.sum(field[0] * kfield[1]),...  7.63 us
    all_to_all x1, waiting for transfers between devices, per_device(): lax.all_to_all(lax.all_to_all(blocks, 'patch', split_axis=0, concat_axis=...  7.33 us
    scatter x1, local copies, waits for them, and re-layouts, per_device(): placed = jnp.zeros((rows_dev, 3, ncol), jnp.bfloat16).at[arrived_rows.res...  6.97 us
    unnamed x47, local copies, waits for them, and re-layouts  6.62 us
  transfers between devices with their start and end apart: 10, of which 5 were waited for; matrix products, arithmetic and copies ran while one was open for 3% of the time, Pallas kernels for 0%

profile of v1, /device:TPU:0, one launch (start us, length us, event | category | flops | bytes accessed | tf_op | source)
XLA Modules:
  0.0 212.7 jit_solution(16230711869968738362)
XLA Ops:
  1.1 1.1 broadcast_multiply_fusion
  2.2 12.3 %gather_fusion = f32[1024]{0:T(1024)S(1)} fusion(f32[2,2,128,256]{3,2,1,0:T(8,128)S(1)} %broadcast_multiply_fusion, s32[1024]{0:T(1024)S(1)} %bitcast.211), kind=kCustom, calls=%fused_computation.clone | custom fusion | bytes 24576 | tf_op jit(solution)/shard_map/jit(take_along_axis)/gather | solution.py:72
  14.6 12.3 %gather_fusion.1 = f32[1024]{0:T(1024)S(1)} fusion(f32[2,2,128,256]{3,2,1,0:T(8,128)S(1)} %broadcast_multiply_fusion, s32[1024]{0:T(1024)S(1)} %bitcast.213), kind=kCustom, calls=%fused_computation.1.clone | custom fusion | bytes 24576 | tf_op jit(solution)/shard_map/jit(take_along_axis)/gather | solution.py:72
  27.1 3.1 %collective-permute-start.2 = (f32[2,2,2,2,256]{4,3,2,1,0:T(2,128)S(1)}, f32[2,2,2,2,256]{4,3,2,1,0:T(2,128)S(1)}, u32[]{:S(2)}, u32[]{:S(2)}) collective-permute-start(f32[2,2,2,2,256]{4,3,2,1,0:T(2,128)S(1)} %pad_maximum_fusion.4), channel_id=1, source_target_pairs={{0,4},{4,8},{8,12},{12,0},{1,5},{5,9},{9,13},{13,1},{2,6},{6,10},{... | collective-permute-start | bytes 49160 | tf_op jit(solution)/shard_map/ppermute | solution.py:15
  30.1 2.1 collective-permute-start.3
  33.0 3.8 %collective-permute-start.1 = (s32[2,2]{1,0:T(2,128)S(1)}, s32[2,2]{1,0:T(2,128)S(1)}, u32[]{:S(2)}, u32[]{:S(2)}) collective-permute-start(s32[2,2]{1,0:T(2,128)S(1)} %pad_add_fusion.4), channel_id=1, source_target_pairs={{0,12},{4,0},{8,4},{12,8},{1,13},{5,1},{9,5},{13,9},{2,14},{6,2},{... | collective-permute-start | bytes 56 | tf_op jit(solution)/shard_map/ppermute | solution.py:15
  37.5 3.2 %all-to-all-start = ((s32[4,4,16]{2,1,0:T(4,128)}), s32[4,4,16]{2,1,0:T(4,128)S(1)}, u32[]{:S(2)}, u32[]{:S(2)}) async-start(s32[4,4,16]{2,1,0:T(4,128)} %reshape.291), calls=%async_computation | async-start | bytes 16384 | tf_op jit(solution)/shard_map/all_to_all | solution.py:166
  46.9 3.2 %all-to-all-start.1 = ((s32[4,4,16]{2,0,1:T(4,128)}), s32[4,4,16]{2,0,1:T(4,128)S(1)}, u32[]{:S(2)}, u32[]{:S(2)}) async-start(s32[4,4,16]{2,0,1:T(4,128)} %copy.28), calls=%async_computation.1 | async-start | bytes 16384 | tf_op jit(solution)/shard_map/all_to_all | solution.py:165
  50.2 3.7 %all-to-all-done.1 = s32[4,4,16]{2,0,1:T(4,128)S(1)} async-done(((s32[4,4,16]{2,0,1:T(4,128)}), s32[4,4,16]{2,0,1:T(4,128)S(1)}, u32[]{:S(2)}, u32[]{:S(2)}) %all-to-all-start.1) | async-done | bytes 1056 | tf_op jit(solution)/shard_map/all_to_all | solution.py:165
  53.9 4.8 %all-to-all-start.2 = ((bf16[4,4,16,3,256]{4,2,1,3,0:T(8,128)(2,1)}), bf16[4,4,16,3,256]{4,2,1,3,0:T(8,128)(2,1)S(1)}, u32[]{:S(2)}, u32[]{:S(2)}) async-start(bf16[4,4,16,3,256]{4,2,1,3,0:T(8,128)(2,1)} %copy.30), calls=%async_computation.2 | async-start | bytes 786432 | tf_op jit(solution)/shard_map/all_to_all | solution.py:159
  59.1 11.2 %all-to-all-done.2 = bf16[4,4,16,3,256]{4,2,1,3,0:T(8,128)(2,1)S(1)} async-done(((bf16[4,4,16,3,256]{4,2,1,3,0:T(8,128)(2,1)}), bf16[4,4,16,3,256]{4,2,1,3,0:T(8,128)(2,1)S(1)}, u32[]{:S(2)}, u32[]{:S(2)}) %all-to-all-start.2) | async-done | bytes 393248 | tf_op jit(solution)/shard_map/all_to_all | solution.py:159
  71.1 3.5 %all-to-all-start.3 = ((bf16[4,4,16,3,256]{4,2,0,3,1:T(8,128)(2,1)}), bf16[4,4,16,3,256]{4,2,0,3,1:T(8,128)(2,1)S(1)}, u32[]{:S(2)}, u32[]{:S(2)}) async-start(bf16[4,4,16,3,256]{4,2,0,3,1:T(8,128)(2,1)} %copy.31), calls=%async_computation.3 | async-start | bytes 786432 | tf_op jit(solution)/shard_map/all_to_all | solution.py:158
  74.7 7.3 %all-to-all-done.3 = bf16[4,4,16,3,256]{4,2,0,3,1:T(8,128)(2,1)S(1)} async-done(((bf16[4,4,16,3,256]{4,2,0,3,1:T(8,128)(2,1)}), bf16[4,4,16,3,256]{4,2,0,3,1:T(8,128)(2,1)S(1)}, u32[]{:S(2)}, u32[]{:S(2)}) %all-to-all-start.3) | async-done | bytes 393248 | tf_op jit(solution)/shard_map/all_to_all | solution.py:158
  82.5 7.0 %scatter_fusion = bf16[256,3,256]{2,1,0:T(4,128)(2,1)S(1)} fusion(bf16[256,3,256]{2,1,0:T(4,128)(2,1)S(1)} %broadcast_in_dim.225, s32[256]{0:T(256)S(1)} %bitcast.261, bf16[256,3,256]{2,1,0:T(4,128)(2,1)S(1)} %copy.33), kind=kCustom, calls=%fused_computation.4 | custom fusion | bytes 1180672 | tf_op jit(solution)/shard_map/scatter | solution.py:176
  90.1 1.2 copy-done.7
  94.0 3.8 %stack.135 = f32[6]{0:T(128)S(1)} concatenate(f32[1]{0:T(128)} %bitcast.30, f32[1]{0:T(128)} %bitcast.32, f32[1]{0:T(128)} %bitcast.34, f32[1]{0:T(128)} %bitcast.36, f32[1]{0:T(128)} %bitcast.38, f32[1]{0:T(128)} %bitcast.39), dimensions={0} | concatenate | bytes 48 | tf_op jit(solution)/shard_map/stack | solution.py:106
  98.0 30.2 %all-reduce.16 = f32[96]{0:T(128)S(1)} all-reduce(f32[96]{0:T(128)S(1)} %dynamic-update-slice), channel_id=2, replica_groups=mesh['groups'=2,'patch'=4,'sub'=2,'half'=2] {'patch','sub','half'}, use_global_device_ids=true, to_apply=%add.16 | all-reduce | flops 96 | bytes 768
  135.4 1.0 fusion.41
  138.0 12.3 %gather_fusion.3 = f32[1024]{0:T(1024)S(1)} fusion(f32[2,2,128,256]{3,2,1,0:T(8,128)S(1)} %get-tuple-element.46, s32[1024]{0:T(1024)S(1)} %bitcast.214), kind=kCustom, calls=%fused_computation.3.clone | custom fusion | bytes 24576 | tf_op jit(solution)/shard_map/jit(take_along_axis)/gather | solution.py:72
  150.3 12.3 %gather_fusion.2 = f32[1024]{0:T(1024)S(1)} fusion(f32[2,2,128,256]{3,2,1,0:T(8,128)S(1)} %get-tuple-element.46, s32[1024]{0:T(1024)S(1)} %bitcast.212), kind=kCustom, calls=%fused_computation.2.clone | custom fusion | bytes 24576 | tf_op jit(solution)/shard_map/jit(take_along_axis)/gather | solution.py:72
  162.9 3.8 %collective-permute-start.5 = (f32[2,2,2,2,256]{4,3,2,1,0:T(2,128)S(1)}, f32[2,2,2,2,256]{4,3,2,1,0:T(2,128)S(1)}, u32[]{:S(2)}, u32[]{:S(2)}) collective-permute-start(f32[2,2,2,2,256]{4,3,2,1,0:T(2,128)S(1)} %pad_maximum_fusion.5), channel_id=1, source_target_pairs={{0,12},{4,0},{8,4},{12,8},{1,13},{5,1},{9,5},{13,9},{2,14},{6,2},{... | collective-permute-start | bytes 49160 | tf_op jit(solution)/shard_map/ppermute | solution.py:15
  167.4 1.1 collective-permute-done.4
  170.8 3.8 %stack.150 = f32[6]{0:T(128)S(1)} concatenate(f32[1]{0:T(128)} %bitcast.60, f32[1]{0:T(128)} %bitcast.62, f32[1]{0:T(128)} %bitcast.63, f32[1]{0:T(128)} %bitcast.65, f32[1]{0:T(128)} %bitcast.67, f32[1]{0:T(128)} %bitcast.68), dimensions={0} | concatenate | bytes 48 | tf_op jit(solution)/shard_map/stack | solution.py:106
  174.9 29.5 %all-reduce.17 = f32[96]{0:T(128)S(1)} all-reduce(f32[96]{0:T(128)S(1)} %dynamic-update-slice.1), channel_id=3, replica_groups=mesh['groups'=2,'patch'=4,'sub'=2,'half'=2] {'patch','sub','half'}, use_global_device_ids=true, to_apply=%add.17 | all-reduce | flops 96 | bytes 768
  (141 shorter events, 20.8 us)
Async XLA Ops:
  0.0 0.7 copy-start.12
  27.1 31.7 %collective-permute-start.2 = (f32[2,2,2,2,256]{4,3,2,1,0:T(2,128)S(1)}, f32[2,2,2,2,256]{4,3,2,1,0:T(2,128)S(1)}, u32[]{:S(2)}, u32[]{:S(2)}) collective-permute-start(f32[2,2,2,2,256]{4,3,2,1,0:T(2,128)S(1)} %pad_maximum_fusion.4), channel_id=1, source_target_pairs={{0,4},{4,8},{8,12},{12,0},{1,5},{5,9},{9,13},{13,1},{2,6},{6,10},{... | collective-permute-start | bytes 49160 | tf_op jit(solution)/shard_map/ppermute | solution.py:15
  30.1 28.7 %collective-permute-start.3 = (f32[2,2,2,2,256]{4,3,2,1,0:T(2,128)S(1)}, f32[2,2,2,2,256]{4,3,2,1,0:T(2,128)S(1)}, u32[]{:S(2)}, u32[]{:S(2)}) collective-permute-start(f32[2,2,2,2,256]{4,3,2,1,0:T(2,128)S(1)} %pad_maximum_fusion.4), channel_id=1, source_target_pairs={{0,12},{4,0},{8,4},{12,8},{1,13},{5,1},{9,5},{13,9},{2,14},{6,2},{... | collective-permute-start | bytes 49160 | tf_op jit(solution)/shard_map/ppermute | solution.py:15
  32.2 0.7 copy-start.13
  32.9 3.9 %copy-start.11 = (s32[256]{0:T(256)S(1)}, s32[256]{0:T(256)}, u32[]{:S(2)}) copy-start(s32[256]{0:T(256)} %param.15) | copy-start | bytes 3076
  32.9 12.8 %collective-permute-start = (s32[2,2]{1,0:T(2,128)S(1)}, s32[2,2]{1,0:T(2,128)S(1)}, u32[]{:S(2)}, u32[]{:S(2)}) collective-permute-start(s32[2,2]{1,0:T(2,128)S(1)} %pad_add_fusion.4), channel_id=1, source_target_pairs={{0,4},{4,8},{8,12},{12,0},{1,5},{5,9},{9,13},{13,1},{2,6},{6,10},{... | collective-permute-start | bytes 56 | tf_op jit(solution)/shard_map/ppermute | solution.py:15
  33.0 12.8 %collective-permute-start.1 = (s32[2,2]{1,0:T(2,128)S(1)}, s32[2,2]{1,0:T(2,128)S(1)}, u32[]{:S(2)}, u32[]{:S(2)}) collective-permute-start(s32[2,2]{1,0:T(2,128)S(1)} %pad_add_fusion.4), channel_id=1, source_target_pairs={{0,12},{4,0},{8,4},{12,8},{1,13},{5,1},{9,5},{13,9},{2,14},{6,2},{... | collective-permute-start | bytes 56 | tf_op jit(solution)/shard_map/ppermute | solution.py:15
  37.5 8.8 %all-to-all-start = ((s32[4,4,16]{2,1,0:T(4,128)}), s32[4,4,16]{2,1,0:T(4,128)S(1)}, u32[]{:S(2)}, u32[]{:S(2)}) async-start(s32[4,4,16]{2,1,0:T(4,128)} %reshape.291), calls=%async_computation | async-start | bytes 16384 | tf_op jit(solution)/shard_map/all_to_all | solution.py:166
  40.8 1.1 copy-start
  41.8 1.0 copy-start.10
  42.8 1.0 copy-start.1
  46.9 7.0 %all-to-all-start.1 = ((s32[4,4,16]{2,0,1:T(4,128)}), s32[4,4,16]{2,0,1:T(4,128)S(1)}, u32[]{:S(2)}, u32[]{:S(2)}) async-start(s32[4,4,16]{2,0,1:T(4,128)} %copy.28), calls=%async_computation.1 | async-start | bytes 16384 | tf_op jit(solution)/shard_map/all_to_all | solution.py:165
  53.9 16.4 %all-to-all-start.2 = ((bf16[4,4,16,3,256]{4,2,1,3,0:T(8,128)(2,1)}), bf16[4,4,16,3,256]{4,2,1,3,0:T(8,128)(2,1)S(1)}, u32[]{:S(2)}, u32[]{:S(2)}) async-start(bf16[4,4,16,3,256]{4,2,1,3,0:T(8,128)(2,1)} %copy.30), calls=%async_computation.2 | async-start | bytes 786432 | tf_op jit(solution)/shard_map/all_to_all | solution.py:159
  71.1 10.9 %all-to-all-start.3 = ((bf16[4,4,16,3,256]{4,2,0,3,1:T(8,128)(2,1)}), bf16[4,4,16,3,256]{4,2,0,3,1:T(8,128)(2,1)S(1)}, u32[]{:S(2)}, u32[]{:S(2)}) async-start(bf16[4,4,16,3,256]{4,2,0,3,1:T(8,128)(2,1)} %copy.31), calls=%async_computation.3 | async-start | bytes 786432 | tf_op jit(solution)/shard_map/all_to_all | solution.py:158
  90.1 1.2 copy-start.7
  90.1 1.6 copy-start.2
  90.1 1.6 copy-start.4
  91.3 1.0 copy-start.6
  136.8 1.0 copy-start.3
  136.8 1.0 copy-start.5
  162.9 5.6 %collective-permute-start.4 = (f32[2,2,2,2,256]{4,3,2,1,0:T(2,128)S(1)}, f32[2,2,2,2,256]{4,3,2,1,0:T(2,128)S(1)}, u32[]{:S(2)}, u32[]{:S(2)}) collective-permute-start(f32[2,2,2,2,256]{4,3,2,1,0:T(2,128)S(1)} %pad_maximum_fusion.5), channel_id=1, source_target_pairs={{0,4},{4,8},{8,12},{12,0},{1,5},{5,9},{9,13},{13,1},{2,6},{6,10},{... | collective-permute-start | bytes 49160 | tf_op jit(solution)/shard_map/ppermute | solution.py:15
  162.9 5.5 %collective-permute-start.5 = (f32[2,2,2,2,256]{4,3,2,1,0:T(2,128)S(1)}, f32[2,2,2,2,256]{4,3,2,1,0:T(2,128)S(1)}, u32[]{:S(2)}, u32[]{:S(2)}) collective-permute-start(f32[2,2,2,2,256]{4,3,2,1,0:T(2,128)S(1)} %pad_maximum_fusion.5), channel_id=1, source_target_pairs={{0,12},{4,0},{8,4},{12,8},{1,13},{5,1},{9,5},{13,9},{2,14},{6,2},{... | collective-permute-start | bytes 49160 | tf_op jit(solution)/shard_map/ppermute | solution.py:15
  168.9 1.0 copy-start.8
  168.9 1.0 copy-start.9
  (1 other events, 0.7 us)
